TPU v7x, 32 devices: a whole 2x2x4 slice. The times are simulated.
32 devices in a mesh: hier: 8 (over y, x, core), col: 4 (over z).
Axes of the slice: x: 2, y: 2, z: 4, core: 2. Of those that a mesh axis runs over, the one named last changes fastest.
Arguments:
- densities: float32 [32, 2, 256, 256], P('hier', None, 'col'), may hold values from -6 to 6
- hamiltonian: float32 [256, 256], replicated, may hold values from -0.35355339 to 0.35355339, as said below
- couplings: float32 [2, 256, 256], replicated, may hold values from -0.088388348 to 0.088388348, as said below
- gamma: float32 [2], replicated, may hold values from 0.005 to 0.05
- coeff: float32 [2, 2], replicated, may hold values from -0.5 to 0.5
- node_count: int32 [8], replicated, may hold values from 2 to 4, as said below
Outputs:
- new_densities: float32 [32, 2, 256, 256], P('hier', None, 'col')
Inputs may be any that keep to these rules, and one draw needn't show every extreme that they name: `node_count`: at least one index of hier holds 4 nodes; every index holds 2 or more. `hamiltonian`: symmetric. `couplings`: each of the two matrices is symmetric.
All inputs are finite; a program needn't handle non-finite values.
Results may differ from a plain program's by a relative error of at most 0.00012.
Values sent between devices are 32-bit elements; how exact they have to be, the bound alone decides.
A program may use at most 64 MiB of HBM per device.

v0:
```python
import jax
import jax.numpy as jnp
from jax import lax
from jax.sharding import PartitionSpec as P

DEPTH2 = 2
step_size = 0.2


def passed_along(block, axis, distance):
    devices = range(lax.axis_size(axis))
    route = [(i - distance, i) for i in devices if i - distance in devices]
    return lax.ppermute(block, axis, route)


def hierarchy(node_count, device, slot):
    shards = node_count.shape[0]
    columns = jnp.arange(shards, dtype=jnp.int32)
    offsets = jnp.cumsum(node_count) - node_count
    live_total = jnp.sum(node_count) // DEPTH2 * DEPTH2

    def lookup(table, which):
        return jnp.sum(jnp.where(which[:, None] == columns[None, :], table[None, :], 0), axis=1)

    index = lookup(offsets, device) + slot
    live = (slot < lookup(node_count, device)) & (index < live_total)
    first = index // DEPTH2
    second = index % DEPTH2
    targets = (index + DEPTH2, index + 1, index - DEPTH2, index - 1)
    allowed = (
        live & (index + DEPTH2 < live_total),
        live & (second + 1 < DEPTH2),
        live & (first > 0),
        live & (second > 0),
    )
    found = []
    for target, valid in zip(targets, allowed):
        owner = jnp.sum((offsets[None, :] <= target[:, None]).astype(jnp.int32), axis=1) - 1
        within = target - lookup(offsets, owner)
        owner_count = lookup(node_count, owner)
        found.append((owner, within, valid, owner_count))
    return (live, first, second, found)


def combine(upward, downward, raise_w, lower_w, real, imag):
    rise = raise_w[:, None, None]
    fall = lower_w[:, None, None]
    part_re = rise * upward[:, 0] + fall * (real * downward[:, 0] - imag * downward[:, 1])
    part_im = rise * upward[:, 1] + fall * (real * downward[:, 1] + imag * downward[:, 0])
    return jnp.stack([part_re, part_im], axis=1)


def mixes(linked, levels, coeff, sign):
    result = []
    for mode in range(2):
        result.append(
            combine(
                linked[mode],
                linked[mode + 2],
                jnp.sqrt(levels[mode] + 1.0),
                jnp.sqrt(levels[mode]),
                coeff[mode, 0],
                sign * coeff[mode, 1],
            )
        )
    return result


def pick(wide, positions, masks):
    return [jnp.take(wide, positions[j], axis=0) * masks[j] for j in range(4)]


def tail_slots(block, start, half):
    return lax.dynamic_slice_in_dim(block, start, half, 0)


def slope(state, left_mat, right_mat, gamma, coeff, layout_info):
    alive, levels, positions, masks, tail_start = layout_info
    half = state.shape[0] // 2
    high = lax.Precision.HIGHEST
    own_cols = lax.all_to_all(state, "col", split_axis=3, concat_axis=2, tiled=True)
    lower = passed_along(
        (tail_slots(state, tail_start, half), tail_slots(own_cols, tail_start, half)), "hier", 1
    )
    upper = passed_along((state[:half], own_cols[:half]), "hier", -1)
    wide_rows = jnp.concatenate([lower[0], state, upper[0]], axis=0)
    wide_cols = jnp.concatenate([lower[1], own_cols, upper[1]], axis=0)
    rights = mixes(pick(wide_rows, positions, masks), levels, coeff, -1.0)
    lefts = mixes(pick(wide_cols, positions, masks), levels, coeff, 1.0)
    col_stack = jnp.concatenate([own_cols] + lefts, axis=2)
    right = jnp.einsum(
        "scij,jk->scik", jnp.concatenate([state] + rights, axis=3), right_mat, precision=high
    )
    left_cols = jnp.einsum("ij,scjk->scik", left_mat, col_stack, precision=high)
    left = lax.all_to_all(left_cols, "col", split_axis=2, concat_axis=3, tiled=True)
    comm = left - right
    damping = (levels[0] * gamma[0] + levels[1] * gamma[1])[:, None, None]
    out_re = comm[:, 1] - damping * state[:, 0]
    out_im = -comm[:, 0] - damping * state[:, 1]
    return jnp.stack([out_re, out_im], axis=1) * alive


def on_device(densities, hamiltonian, couplings, gamma, coeff, node_count):
    width = densities.shape[0]
    half = width // 2
    here = lax.axis_index("hier")
    device = jnp.full((width,), here, jnp.int32)
    slot = jnp.arange(width, dtype=jnp.int32)
    live, first, second, found = hierarchy(node_count, device, slot)
    own_count = jnp.sum(
        jnp.where(jnp.arange(node_count.shape[0], dtype=jnp.int32) == here, node_count, 0)
    )
    tail_start = own_count - half
    positions = []
    for o, w, v, c in found:
        place = jnp.where(
            o == here, half + w, jnp.where(o < here, w - (c - half), half + width + w)
        )
        positions.append(jnp.where(v, place, 0))
    masks = [v.astype(jnp.float32)[:, None, None, None] for o, w, v, c in found]
    levels = (first.astype(jnp.float32), second.astype(jnp.float32))
    alive = live.astype(jnp.float32)[:, None, None, None]
    layout_info = (alive, levels, positions, masks, tail_start)
    left_mat = jnp.concatenate([hamiltonian, couplings[0], couplings[1]], axis=1)
    right_mat = jnp.concatenate([hamiltonian, couplings[0], couplings[1]], axis=0)
    first_slope = slope(densities, left_mat, right_mat, gamma, coeff, layout_info)
    middle = densities + 0.5 * step_size * first_slope
    second_slope = slope(middle, left_mat, right_mat, gamma, coeff, layout_info)
    return densities + step_size * second_slope


def solution(mesh):
    placed = (P("hier", None, "col", None), P(), P(), P(), P(), P())
    return jax.shard_map(
        on_device,
        mesh=mesh,
        in_specs=placed,
        out_specs=P("hier", None, "col", None),
        check_vma=False,
    )
```

profile of v0, /device:TPU:3, one launch (start us, length us, event | category | flops | bytes accessed | tf_op | source)
XLA Modules:
  0.0 187.6 jit_solution(3273176700388385365)
XLA Ops:
  0.0 1.5 copy.27
  1.6 1.8 reshape.390
  3.3 4.7 %all-to-all-start = ((f32[4,1,32768]{2,1,0:T(1,128)}), f32[4,1,32768]{2,1,0:T(1,128)S(1)}, u32[]{:S(2)}, u32[]{:S(2)}) async-start(f32[4,1,32768]{2,1,0:T(1,128)} %reshape.390), calls=%async_computation | async-start | bytes 1048576 | tf_op jit(solution)/shard_map/all_to_all | solution.py:81
  10.3 4.0 %collective-permute-start.2 = (f32[2,2,64,256]{3,2,1,0:T(8,128)S(1)}, f32[2,2,64,256]{3,2,1,0:T(8,128)S(1)}, u32[]{:S(2)}, u32[]{:S(2)}) collective-permute-start(f32[2,2,64,256]{3,2,1,0:T(8,128)S(1)} %get-tuple-element.57), channel_id=1, source_target_pairs={{0,4},{4,8},{8,12},{12,16},{16,20},{20,24},{24,28},{1,5},{5,9},{9,... | collective-permute-start | bytes 786440 | tf_op jit(solution)/shard_map/ppermute | solution.py:13
  14.2 1.9 %collective-permute-start.3 = (f32[2,2,64,256]{3,2,1,0:T(8,128)S(1)}, f32[2,2,64,256]{3,2,1,0:T(8,128)S(1)}, u32[]{:S(2)}, u32[]{:S(2)}) collective-permute-start(f32[2,2,64,256]{3,2,1,0:T(8,128)S(1)} %get-tuple-element.56), channel_id=1, source_target_pairs={{4,0},{8,4},{12,8},{16,12},{20,16},{24,20},{28,24},{5,1},{9,5},{13... | collective-permute-start | bytes 786440 | tf_op jit(solution)/shard_map/ppermute | solution.py:13
  24.2 1.4 gather_fusion.6
  26.1 2.0 %reduce = f32[4,32768]{1,0:T(4,128)S(1)} reduce(f32[4,1,32768]{2,1,0:T(1,128)S(1)} %all-to-all-done, f32[]{:T(128)} %broadcast.622), dimensions={1}, to_apply=%all_to_all.52.reduce_sub_computation | reduce | bytes 1048580 | tf_op jit(solution)/shard_map/all_to_all | solution.py:81
  28.1 1.7 reshape.391
  29.8 1.9 %copy.44 = f32[4,2,64,4,64]{2,3,4,1,0:T(4,128)S(1)} copy(f32[4,2,64,4,64]{2,0,1,4,3:T(4,128)} %bitcast.69) | data formatting | bytes 1048576 | tf_op jit(solution)/shard_map/all_to_all | solution.py:81
  33.1 4.5 %collective-permute-start = (f32[2,2,256,64]{2,3,1,0:T(8,128)}, f32[2,2,256,64]{2,3,1,0:T(8,128)}, u32[]{:S(2)}, u32[]{:S(2)}) collective-permute-start(f32[2,2,256,64]{2,3,1,0:T(8,128)} %constant_dynamic-slice_fusion.2), channel_id=1, source_target_pairs={{0,4},{4,8},{8,12},{12,16},{16,20},{20,24},{24,28},{1,5},{5,9},{9,... | collective-permute-start | bytes 786440 | tf_op jit(solution)/shard_map/ppermute | solution.py:13
  37.7 2.0 %select_multiply_fusion.9 = f32[4,2,64,256]{3,2,1,0:T(8,128)} fusion(f32[4,2,64,256]{3,2,1,0:T(8,128)} %gather_fusion.6, f32[4]{0:T(128)S(1)} %get-tuple-element.73, pred[4]{0:T(512)(128)(4,1)S(1)} %get-tuple-element.68), kind=kLoop, calls=%fused_computation.82 | loop fusion | flops 262144 | bytes 1048596 | tf_op jit(solution)/shard_map/mul | solution.py:70
  39.6 1.4 gather_fusion.7
  41.8 1.4 slice.195
  43.3 1.9 %collective-permute-start.1 = (f32[2,2,256,64]{2,3,1,0:T(8,128)S(1)}, f32[2,2,256,64]{2,3,1,0:T(8,128)}, u32[]{:S(2)}, u32[]{:S(2)}) collective-permute-start(f32[2,2,256,64]{2,3,1,0:T(8,128)S(1)} %slice.195), channel_id=1, source_target_pairs={{4,0},{8,4},{12,8},{16,12},{20,16},{24,20},{28,24},{5,1},{9,5},{13... | collective-permute-start | bytes 786440 | tf_op jit(solution)/shard_map/ppermute | solution.py:13
  46.1 1.4 gather_fusion.4
  48.6 3.4 %collective-permute-done.1 = f32[2,2,256,64]{2,3,1,0:T(8,128)} collective-permute-done((f32[2,2,256,64]{2,3,1,0:T(8,128)S(1)}, f32[2,2,256,64]{2,3,1,0:T(8,128)}, u32[]{:S(2)}, u32[]{:S(2)}) %collective-permute-start.1) | collective-permute-done | bytes 262176 | tf_op jit(solution)/shard_map/ppermute | solution.py:13
  52.9 1.4 gather_fusion.2
  54.3 1.4 gather_fusion.3
  56.3 2.0 %select_multiply_fusion.13 = f32[4,2,256,64]{2,3,1,0:T(8,128)} fusion(f32[4,2,256,64]{2,3,1,0:T(8,128)} %gather_fusion.2, f32[4]{0:T(128)S(1)} %get-tuple-element.73, pred[4]{0:T(512)(128)(4,1)S(1)} %get-tuple-element.68), kind=kLoop, calls=%fused_computation.86 | loop fusion | flops 262144 | bytes 1048596 | tf_op jit(solution)/shard_map/mul | solution.py:70
  59.2 1.4 gather_fusion.1
  63.3 1.6 fusion.74
  65.0 1.4 fusion.43
  67.2 1.9 %reshape.392 = f32[4,1,32768]{2,1,0:T(1,128)} reshape(f32[256,4,2,64]{3,2,1,0:T(2,128)S(1)} %bitcast.65) | data formatting | bytes 1048576
  69.1 4.9 %all-to-all-start.1 = ((f32[4,1,32768]{2,1,0:T(1,128)}), f32[4,1,32768]{2,1,0:T(1,128)}, u32[]{:S(2)}, u32[]{:S(2)}) async-start(f32[4,1,32768]{2,1,0:T(1,128)} %reshape.392), calls=%async_computation.1 | async-start | bytes 1048576 | tf_op jit(solution)/shard_map/all_to_all | solution.py:95
  74.2 1.4 gather_fusion.5
  76.8 1.5 fusion.68
  78.3 1.6 fusion.70
  79.9 6.6 %all-to-all-done.1 = f32[4,1,32768]{2,1,0:T(1,128)} async-done(((f32[4,1,32768]{2,1,0:T(1,128)}), f32[4,1,32768]{2,1,0:T(1,128)}, u32[]{:S(2)}, u32[]{:S(2)}) %all-to-all-start.1) | async-done | bytes 524320 | tf_op jit(solution)/shard_map/all_to_all | solution.py:95
  86.5 3.0 %reduce.1 = f32[4,32768]{1,0:T(4,128)S(1)} reduce(f32[4,1,32768]{2,1,0:T(1,128)} %all-to-all-done.1, f32[]{:T(128)} %broadcast.622), dimensions={1}, to_apply=%all_to_all.56.reduce_sub_computation | reduce | bytes 1048580 | tf_op jit(solution)/shard_map/all_to_all | solution.py:95
  92.2 2.4 %fusion.49 = f32[4,2,64,256]{3,2,1,0:T(8,128)S(1)} fusion(f32[4,2,64,256]{3,2,1,0:T(8,128)S(1)} %all_to_all.59, f32[4,1,64,256]{3,2,1,0:T(8,128)S(1)} %copy-done.29, f32[4,1,64,256]{3,2,1,0:T(8,128)S(1)} %copy-done.28, f32[4,1,64,256]{3,2,1,0:T(8,128)} %get-tuple-element.43, f32[4,1,64,256]{3,2,1,0:T(8,128)S(1)} %copy-done.30, ...), kind=kOutput, calls=%fused_computation.59 | convolution fusion | flops 1210056704 | bytes 3407872 | tf_op jit(solution)/shard_map/scij,jk->scik/dot_general | solution.py:91
  95.6 1.9 %reshape.394 = f32[4,1,32768]{2,1,0:T(1,128)} reshape(f32[256,4,2,64]{3,2,1,0:T(2,128)S(1)} %bitcast.68) | data formatting | bytes 1048576
  97.5 3.5 %all-to-all-start.2 = ((f32[4,1,32768]{2,1,0:T(1,128)}), f32[4,1,32768]{2,1,0:T(1,128)S(1)}, u32[]{:S(2)}, u32[]{:S(2)}) async-start(f32[4,1,32768]{2,1,0:T(1,128)} %reshape.394), calls=%async_computation.2 | async-start | bytes 1048576 | tf_op jit(solution)/shard_map/all_to_all | solution.py:81
  101.1 1.9 %collective-permute-start.7 = (f32[2,2,64,256]{3,2,1,0:T(8,128)S(1)}, f32[2,2,64,256]{3,2,1,0:T(8,128)S(1)}, u32[]{:S(2)}, u32[]{:S(2)}) collective-permute-start(f32[2,2,64,256]{3,2,1,0:T(8,128)S(1)} %get-tuple-element.55), channel_id=1, source_target_pairs={{4,0},{8,4},{12,8},{16,12},{20,16},{24,20},{28,24},{5,1},{9,5},{13... | collective-permute-start | bytes 786440 | tf_op jit(solution)/shard_map/ppermute | solution.py:13
  103.0 4.5 %collective-permute-start.6 = (f32[2,2,64,256]{3,2,1,0:T(8,128)S(1)}, f32[2,2,64,256]{3,2,1,0:T(8,128)S(1)}, u32[]{:S(2)}, u32[]{:S(2)}) collective-permute-start(f32[2,2,64,256]{3,2,1,0:T(8,128)S(1)} %get-tuple-element.54), channel_id=1, source_target_pairs={{0,4},{4,8},{8,12},{12,16},{16,20},{20,24},{24,28},{1,5},{5,9},{9,... | collective-permute-start | bytes 786440 | tf_op jit(solution)/shard_map/ppermute | solution.py:13
  107.5 3.4 %collective-permute-done.7 = f32[2,2,64,256]{3,2,1,0:T(8,128)S(1)} collective-permute-done((f32[2,2,64,256]{3,2,1,0:T(8,128)S(1)}, f32[2,2,64,256]{3,2,1,0:T(8,128)S(1)}, u32[]{:S(2)}, u32[]{:S(2)}) %collective-permute-start.7) | collective-permute-done | bytes 262176 | tf_op jit(solution)/shard_map/ppermute | solution.py:13
  111.0 1.4 gather_fusion.14
  112.4 3.5 %all-to-all-done.2 = f32[4,1,32768]{2,1,0:T(1,128)S(1)} async-done(((f32[4,1,32768]{2,1,0:T(1,128)}), f32[4,1,32768]{2,1,0:T(1,128)S(1)}, u32[]{:S(2)}, u32[]{:S(2)}) %all-to-all-start.2) | async-done | bytes 524320 | tf_op jit(solution)/shard_map/all_to_all | solution.py:81
  115.9 2.0 %reduce.2 = f32[4,32768]{1,0:T(4,128)S(1)} reduce(f32[4,1,32768]{2,1,0:T(1,128)S(1)} %all-to-all-done.2, f32[]{:T(128)} %broadcast.622), dimensions={1}, to_apply=%all_to_all.60.reduce_sub_computation | reduce | bytes 1048580 | tf_op jit(solution)/shard_map/all_to_all | solution.py:81
  118.0 1.8 reshape.395
  119.8 1.9 %copy.42 = f32[4,2,64,4,64]{2,3,4,1,0:T(4,128)S(1)} copy(f32[4,2,64,4,64]{2,1,0,4,3:T(2,128)} %bitcast.72) | data formatting | bytes 1048576 | tf_op jit(solution)/shard_map/all_to_all | solution.py:81
  121.7 1.4 all_to_all.63
  123.1 1.7 constant_dynamic-slice_fusion
  124.8 3.7 %collective-permute-start.4 = (f32[2,2,256,64]{2,3,1,0:T(8,128)}, f32[2,2,256,64]{2,3,1,0:T(8,128)}, u32[]{:S(2)}, u32[]{:S(2)}) collective-permute-start(f32[2,2,256,64]{2,3,1,0:T(8,128)} %constant_dynamic-slice_fusion), channel_id=1, source_target_pairs={{0,4},{4,8},{8,12},{12,16},{16,20},{20,24},{24,28},{1,5},{5,9},{9,... | collective-permute-start | bytes 786440 | tf_op jit(solution)/shard_map/ppermute | solution.py:13
  128.4 2.0 %select_multiply_fusion.1 = f32[4,2,64,256]{3,2,1,0:T(8,128)} fusion(f32[4,2,64,256]{3,2,1,0:T(8,128)} %gather_fusion.14, f32[4]{0:T(128)S(1)} %get-tuple-element.73, pred[4]{0:T(512)(128)(4,1)S(1)} %get-tuple-element.68), kind=kLoop, calls=%fused_computation.74 | loop fusion | flops 262144 | bytes 1048596 | tf_op jit(solution)/shard_map/mul | solution.py:70
  130.4 1.4 gather_fusion.15
  132.6 1.4 slice.226
  134.0 1.9 %collective-permute-start.5 = (f32[2,2,256,64]{2,3,1,0:T(8,128)S(1)}, f32[2,2,256,64]{2,3,1,0:T(8,128)}, u32[]{:S(2)}, u32[]{:S(2)}) collective-permute-start(f32[2,2,256,64]{2,3,1,0:T(8,128)S(1)} %slice.226), channel_id=1, source_target_pairs={{4,0},{8,4},{12,8},{16,12},{20,16},{24,20},{28,24},{5,1},{9,5},{13... | collective-permute-start | bytes 786440 | tf_op jit(solution)/shard_map/ppermute | solution.py:13
  136.9 1.4 gather_fusion.12
  140.3 2.4 %collective-permute-done.5 = f32[2,2,256,64]{2,3,1,0:T(8,128)} collective-permute-done((f32[2,2,256,64]{2,3,1,0:T(8,128)S(1)}, f32[2,2,256,64]{2,3,1,0:T(8,128)}, u32[]{:S(2)}, u32[]{:S(2)}) %collective-permute-start.5) | collective-permute-done | bytes 262176 | tf_op jit(solution)/shard_map/ppermute | solution.py:13
  143.7 1.4 gather_fusion.10
  145.1 1.4 gather_fusion.11
  146.5 1.4 gather_fusion.8
  147.9 1.4 gather_fusion.9
  153.1 1.6 fusion.65
  154.7 2.2 %fusion.40 = f32[4,2,256,64]{2,3,1,0:T(8,128)} fusion(f32[4,1,256,64]{2,3,1,0:T(8,128)S(1)} %get-tuple-element.41, f32[4,1,256,64]{2,3,1,0:T(8,128)S(1)} %get-tuple-element.40, f32[4,1,256,64]{2,3,1,0:T(8,128)S(1)} %get-tuple-element.39, f32[4,1,256,64]{2,3,1,0:T(8,128)S(1)} %get-tuple-element.38, f32[4,2,256,64]{2,3,1,0:T(8,128)S(1)} %copy-done.6, ...), kind=kOutput, calls=%fused_computation.56 | convolution fusion | flops 1209925632 | bytes 2883584 | tf_op jit(solution)/shard_map/ij,scjk->scik/dot_general | solution.py:94
  157.0 1.7 copy.33
  158.6 1.9 %reshape.396 = f32[4,1,32768]{2,1,0:T(1,128)} reshape(f32[256,4,2,64]{3,2,1,0:T(2,128)S(1)} %bitcast.66) | data formatting | bytes 1048576
  160.5 4.3 %all-to-all-start.3 = ((f32[4,1,32768]{2,1,0:T(1,128)}), f32[4,1,32768]{2,1,0:T(1,128)}, u32[]{:S(2)}, u32[]{:S(2)}) async-start(f32[4,1,32768]{2,1,0:T(1,128)} %reshape.396), calls=%async_computation.3 | async-start | bytes 1048576 | tf_op jit(solution)/shard_map/all_to_all | solution.py:95
  165.7 1.4 gather_fusion.13
  168.3 1.6 fusion.59
  169.9 1.6 fusion.61
  171.5 6.9 %all-to-all-done.3 = f32[4,1,32768]{2,1,0:T(1,128)} async-done(((f32[4,1,32768]{2,1,0:T(1,128)}), f32[4,1,32768]{2,1,0:T(1,128)}, u32[]{:S(2)}, u32[]{:S(2)}) %all-to-all-start.3) | async-done | bytes 524320 | tf_op jit(solution)/shard_map/all_to_all | solution.py:95
  178.4 3.0 %reduce.3 = f32[4,32768]{1,0:T(4,128)S(1)} reduce(f32[4,1,32768]{2,1,0:T(1,128)} %all-to-all-done.3, f32[]{:T(128)} %broadcast.622), dimensions={1}, to_apply=%all_to_all.64.reduce_sub_computation | reduce | bytes 1048580 | tf_op jit(solution)/shard_map/all_to_all | solution.py:95
  183.9 2.6 %fusion.46 = f32[4,2,64,256]{3,2,1,0:T(8,128)S(1)} fusion(f32[4,2,64,256]{3,2,1,0:T(8,128)S(1)} %all_to_all.67, f32[4,1,64,256]{3,2,1,0:T(8,128)} %get-tuple-element.37, f32[4,1,64,256]{3,2,1,0:T(8,128)S(1)} %copy-done.27, f32[4,1,64,256]{3,2,1,0:T(8,128)} %get-tuple-element.35, f32[4,1,64,256]{3,2,1,0:T(8,128)} %get-tuple-element.34, ...), kind=kOutput, calls=%fused_computation.58 | convolution fusion | flops 1210056704 | bytes 3407872 | tf_op jit(solution)/shard_map/scij,jk->scik/dot_general | solution.py:91
  (145 shorter events, 35.1 us)
Async XLA Ops:
  1.5 6.5 %copy-start.31 = (s32[8]{0:T(128)S(1)}, s32[8]{0:T(128)}, u32[]{:S(2)}) copy-start(s32[8]{0:T(128)} %param.15) | copy-start | bytes 100
  1.6 8.6 %copy-start = (f32[4,2,64,256]{3,2,1,0:T(8,128)S(1)}, f32[4,2,64,256]{3,2,1,0:T(8,128)}, u32[]{:S(2)}) copy-start(f32[4,2,64,256]{3,2,1,0:T(8,128)} %param.10) | copy-start | bytes 1572868
  3.3 15.4 %copy-start.33 = (f32[2]{0:T(128)S(1)}, f32[2]{0:T(128)}, u32[]{:S(2)}) copy-start(f32[2]{0:T(128)} %param.13) | copy-start | bytes 28
  3.3 17.9 %copy-start.20 = (f32[2,256,256]{2,1,0:T(8,128)S(1)}, f32[2,256,256]{2,1,0:T(8,128)}, u32[]{:S(2)}) copy-start(f32[2,256,256]{2,1,0:T(8,128)} %param.12) | copy-start | bytes 1572868
  3.3 22.3 %all-to-all-start = ((f32[4,1,32768]{2,1,0:T(1,128)}), f32[4,1,32768]{2,1,0:T(1,128)S(1)}, u32[]{:S(2)}, u32[]{:S(2)}) async-start(f32[4,1,32768]{2,1,0:T(1,128)} %reshape.390), calls=%async_computation | async-start | bytes 1048576 | tf_op jit(solution)/shard_map/all_to_all | solution.py:81
  10.2 11.9 %copy-start.32 = (f32[2,2]{1,0:T(2,128)S(1)}, f32[2,2]{1,0:T(2,128)}, u32[]{:S(2)}) copy-start(f32[2,2]{1,0:T(2,128)} %param.14) | copy-start | bytes 52
  10.3 13.8 %collective-permute-start.2 = (f32[2,2,64,256]{3,2,1,0:T(8,128)S(1)}, f32[2,2,64,256]{3,2,1,0:T(8,128)S(1)}, u32[]{:S(2)}, u32[]{:S(2)}) collective-permute-start(f32[2,2,64,256]{3,2,1,0:T(8,128)S(1)} %get-tuple-element.57), channel_id=1, source_target_pairs={{0,4},{4,8},{8,12},{12,16},{16,20},{20,24},{24,28},{1,5},{5,9},{9,... | collective-permute-start | bytes 786440 | tf_op jit(solution)/shard_map/ppermute | solution.py:13
  14.2 10.0 %collective-permute-start.3 = (f32[2,2,64,256]{3,2,1,0:T(8,128)S(1)}, f32[2,2,64,256]{3,2,1,0:T(8,128)S(1)}, u32[]{:S(2)}, u32[]{:S(2)}) collective-permute-start(f32[2,2,64,256]{3,2,1,0:T(8,128)S(1)} %get-tuple-element.56), channel_id=1, source_target_pairs={{4,0},{8,4},{12,8},{16,12},{20,16},{24,20},{28,24},{5,1},{9,5},{13... | collective-permute-start | bytes 786440 | tf_op jit(solution)/shard_map/ppermute | solution.py:13
  32.4 16.2 %copy-start.7 = (f32[4,2,256,64]{2,3,1,0:T(8,128)}, f32[4,2,256,64]{2,3,1,0:T(8,128)S(1)}, u32[]{:S(2)}) copy-start(f32[4,2,256,64]{2,3,1,0:T(8,128)S(1)} %all_to_all.55) | copy-start | bytes 1572868
  33.1 14.4 %collective-permute-start = (f32[2,2,256,64]{2,3,1,0:T(8,128)}, f32[2,2,256,64]{2,3,1,0:T(8,128)}, u32[]{:S(2)}, u32[]{:S(2)}) collective-permute-start(f32[2,2,256,64]{2,3,1,0:T(8,128)} %constant_dynamic-slice_fusion.2), channel_id=1, source_target_pairs={{0,4},{4,8},{8,12},{12,16},{16,20},{20,24},{24,28},{1,5},{5,9},{9,... | collective-permute-start | bytes 786440 | tf_op jit(solution)/shard_map/ppermute | solution.py:13
  41.8 3.4 %copy-start.18 = (f32[4,2,64,256]{3,2,1,0:T(8,128)S(1)}, f32[4,2,64,256]{3,2,1,0:T(8,128)}, u32[]{:S(2)}) copy-start(f32[4,2,64,256]{3,2,1,0:T(8,128)} %gather_fusion.7) | copy-start | bytes 1572868
  43.3 8.7 %collective-permute-start.1 = (f32[2,2,256,64]{2,3,1,0:T(8,128)S(1)}, f32[2,2,256,64]{2,3,1,0:T(8,128)}, u32[]{:S(2)}, u32[]{:S(2)}) collective-permute-start(f32[2,2,256,64]{2,3,1,0:T(8,128)S(1)} %slice.195), channel_id=1, source_target_pairs={{4,0},{8,4},{12,8},{16,12},{20,16},{24,20},{28,24},{5,1},{9,5},{13... | collective-permute-start | bytes 786440 | tf_op jit(solution)/shard_map/ppermute | solution.py:13
  56.3 2.0 %copy-start.5 = (f32[4,2,256,64]{2,3,1,0:T(8,128)S(1)}, f32[4,2,256,64]{2,3,1,0:T(8,128)}, u32[]{:S(2)}) copy-start(f32[4,2,256,64]{2,3,1,0:T(8,128)} %gather_fusion.3) | copy-start | bytes 1572868
  60.6 1.0 copy-start.4
  60.6 1.2 copy-start.14
  60.6 1.4 copy-start.15
  63.3 1.6 copy-start.8
  63.3 1.6 copy-start.21
  63.3 1.6 copy-start.23
  63.3 1.6 copy-start.34
  69.1 4.9 %copy-start.17 = (f32[4,2,64,256]{3,2,1,0:T(8,128)S(1)}, f32[4,2,64,256]{3,2,1,0:T(8,128)}, u32[]{:S(2)}) copy-start(f32[4,2,64,256]{3,2,1,0:T(8,128)} %gather_fusion.4) | copy-start | bytes 1572868
  69.1 17.4 %all-to-all-start.1 = ((f32[4,1,32768]{2,1,0:T(1,128)}), f32[4,1,32768]{2,1,0:T(1,128)}, u32[]{:S(2)}, u32[]{:S(2)}) async-start(f32[4,1,32768]{2,1,0:T(1,128)} %reshape.392), calls=%async_computation.1 | async-start | bytes 1048576 | tf_op jit(solution)/shard_map/all_to_all | solution.py:95
  74.2 2.6 %copy-start.11 = (f32[4,2,64,256]{3,2,1,0:T(8,128)S(1)}, f32[4,2,64,256]{3,2,1,0:T(8,128)}, u32[]{:S(2)}) copy-start(f32[4,2,64,256]{3,2,1,0:T(8,128)} %select_multiply_fusion.9) | copy-start | bytes 1572868
  74.2 2.6 %copy-start.12 = (f32[4,2,64,256]{3,2,1,0:T(8,128)S(1)}, f32[4,2,64,256]{3,2,1,0:T(8,128)}, u32[]{:S(2)}) copy-start(f32[4,2,64,256]{3,2,1,0:T(8,128)} %select_multiply_fusion.8) | copy-start | bytes 1572868
  91.0 1.0 copy-start.24
  91.0 1.0 copy-start.28
  91.0 1.1 copy-start.29
  91.0 1.2 copy-start.30
  97.5 18.4 %all-to-all-start.2 = ((f32[4,1,32768]{2,1,0:T(1,128)}), f32[4,1,32768]{2,1,0:T(1,128)S(1)}, u32[]{:S(2)}, u32[]{:S(2)}) async-start(f32[4,1,32768]{2,1,0:T(1,128)} %reshape.394), calls=%async_computation.2 | async-start | bytes 1048576 | tf_op jit(solution)/shard_map/all_to_all | solution.py:81
  101.1 9.8 %collective-permute-start.7 = (f32[2,2,64,256]{3,2,1,0:T(8,128)S(1)}, f32[2,2,64,256]{3,2,1,0:T(8,128)S(1)}, u32[]{:S(2)}, u32[]{:S(2)}) collective-permute-start(f32[2,2,64,256]{3,2,1,0:T(8,128)S(1)} %get-tuple-element.55), channel_id=1, source_target_pairs={{4,0},{8,4},{12,8},{16,12},{20,16},{24,20},{28,24},{5,1},{9,5},{13... | collective-permute-start | bytes 786440 | tf_op jit(solution)/shard_map/ppermute | solution.py:13
  103.0 7.9 %collective-permute-start.6 = (f32[2,2,64,256]{3,2,1,0:T(8,128)S(1)}, f32[2,2,64,256]{3,2,1,0:T(8,128)S(1)}, u32[]{:S(2)}, u32[]{:S(2)}) collective-permute-start(f32[2,2,64,256]{3,2,1,0:T(8,128)S(1)} %get-tuple-element.54), channel_id=1, source_target_pairs={{0,4},{4,8},{8,12},{12,16},{16,20},{20,24},{24,28},{1,5},{5,9},{9,... | collective-permute-start | bytes 786440 | tf_op jit(solution)/shard_map/ppermute | solution.py:13
  124.8 13.5 %collective-permute-start.4 = (f32[2,2,256,64]{2,3,1,0:T(8,128)}, f32[2,2,256,64]{2,3,1,0:T(8,128)}, u32[]{:S(2)}, u32[]{:S(2)}) collective-permute-start(f32[2,2,256,64]{2,3,1,0:T(8,128)} %constant_dynamic-slice_fusion), channel_id=1, source_target_pairs={{0,4},{4,8},{8,12},{12,16},{16,20},{20,24},{24,28},{1,5},{5,9},{9,... | collective-permute-start | bytes 786440 | tf_op jit(solution)/shard_map/ppermute | solution.py:13
  132.6 3.4 %copy-start.19 = (f32[4,2,64,256]{3,2,1,0:T(8,128)S(1)}, f32[4,2,64,256]{3,2,1,0:T(8,128)}, u32[]{:S(2)}) copy-start(f32[4,2,64,256]{3,2,1,0:T(8,128)} %gather_fusion.15) | copy-start | bytes 1572868
  134.0 8.7 %collective-permute-start.5 = (f32[2,2,256,64]{2,3,1,0:T(8,128)S(1)}, f32[2,2,256,64]{2,3,1,0:T(8,128)}, u32[]{:S(2)}, u32[]{:S(2)}) collective-permute-start(f32[2,2,256,64]{2,3,1,0:T(8,128)S(1)} %slice.226), channel_id=1, source_target_pairs={{4,0},{8,4},{12,8},{16,12},{20,16},{24,20},{28,24},{5,1},{9,5},{13... | collective-permute-start | bytes 786440 | tf_op jit(solution)/shard_map/ppermute | solution.py:13
  149.3 1.3 copy-start.1
  149.3 1.4 copy-start.2
  150.5 1.1 copy-start.3
  153.0 1.6 copy-start.6
  153.1 1.6 copy-start.22
  153.1 1.6 copy-start.25
  153.1 1.6 copy-start.35
  160.5 4.3 %copy-start.16 = (f32[4,2,64,256]{3,2,1,0:T(8,128)S(1)}, f32[4,2,64,256]{3,2,1,0:T(8,128)}, u32[]{:S(2)}) copy-start(f32[4,2,64,256]{3,2,1,0:T(8,128)} %gather_fusion.12) | copy-start | bytes 1572868
  160.5 17.9 %all-to-all-start.3 = ((f32[4,1,32768]{2,1,0:T(1,128)}), f32[4,1,32768]{2,1,0:T(1,128)}, u32[]{:S(2)}, u32[]{:S(2)}) async-start(f32[4,1,32768]{2,1,0:T(1,128)} %reshape.396), calls=%async_computation.3 | async-start | bytes 1048576 | tf_op jit(solution)/shard_map/all_to_all | solution.py:95
  165.7 2.5 %copy-start.9 = (f32[4,2,64,256]{3,2,1,0:T(8,128)S(1)}, f32[4,2,64,256]{3,2,1,0:T(8,128)}, u32[]{:S(2)}) copy-start(f32[4,2,64,256]{3,2,1,0:T(8,128)} %select_multiply_fusion.1) | copy-start | bytes 1572868
  165.7 2.6 %copy-start.10 = (f32[4,2,64,256]{3,2,1,0:T(8,128)S(1)}, f32[4,2,64,256]{3,2,1,0:T(8,128)}, u32[]{:S(2)}) copy-start(f32[4,2,64,256]{3,2,1,0:T(8,128)} %select_multiply_fusion) | copy-start | bytes 1572868
  168.3 1.6 copy-start.13
  182.9 1.0 copy-start.26
  182.9 1.0 copy-start.27
where the time goes:
time: 189 us; the launch traced here: 188 us
  local copies, waits for them, and re-layouts  64.8 us (34%)
  starting transfers between devices  41.8 us (22%)
  other arithmetic  40.4 us (21%)
  waiting for transfers between devices  26.2 us (14%)
  matrix products  8.67 us (5%)
  between operations  5.74 us (3%)
    ppermute x8, starting transfers between devices, passed_along(): return lax.ppermute(block, axis, route)  24.4 us
    gather x16, local copies, waits for them, and re-layouts, pick(): return [jnp.take(wide, positions[j], axis=0) * masks[j] for j in range(4)]  21.4 us
    unnamed x87, local copies, waits for them, and re-layouts  20.2 us
    mul x16, other arithmetic, pick(): return [jnp.take(wide, positions[j], axis=0) * masks[j] for j in range(4)]  13.8 us
    all_to_all x2, waiting for transfers between devices, slope(): lax.all_to_all(left_cols, 'col', split_axis=2, concat_axis=3, tiled=True)  13.5 us
    add x8, other arithmetic, combine(): rise * upward[:, 0] + fall * (real * downward[:, 0] - imag * downward[:, 1])  12.2 us
    all_to_all x2, starting transfers between devices, slope(): lax.all_to_all(left_cols, 'col', split_axis=2, concat_axis=3, tiled=True)  9.21 us
    ppermute x8, waiting for transfers between devices, passed_along(): return lax.ppermute(block, axis, route)  9.18 us
  transfers between devices with their start and end apart: 12, of which 6 were waited for; matrix products, arithmetic and copies ran while one was open for 21% of the time, Pallas kernels for 0%

commit v1 on v0

--- a/solution.py
+++ b/solution.py
@@ -78,7 +78,10 @@
     alive, levels, positions, masks, tail_start = layout_info
     half = state.shape[0] // 2
     high = lax.Precision.HIGHEST
-    own_cols = lax.all_to_all(state, "col", split_axis=3, concat_axis=2, tiled=True)
+    peers = lax.axis_size("col")
+    blocks = jnp.stack(jnp.split(state, peers, axis=3), axis=0)
+    blocks = lax.all_to_all(blocks, "col", split_axis=0, concat_axis=0)
+    own_cols = jnp.concatenate(blocks, axis=2)
     lower = passed_along(
         (tail_slots(state, tail_start, half), tail_slots(own_cols, tail_start, half)), "hier", 1
     )

time: 189 us -> 190 us (level)
    reshape x0 -> x4, local copies, waits for them, and re-layouts: none -> 7.12 us  [slope(): own_cols = jnp.concatenate(blocks, axis=2)]
    all_to_all x5 -> x1, local copies, waits for them, and re-layouts: 6.31 us -> 0.59 us  [slope(): blocks = lax.all_to_all(blocks, 'col', split_axis=0, concat_axis=0)]
    unnamed x87 -> x86, local copies, waits for them, and re-layouts: 20.2 us -> 16.5 us
    slice x5 -> x7, local copies, waits for them, and re-layouts: 4.56 us -> 5.04 us  [slope(): upper = passed_along((state[:half], own_cols[:half]), 'hier', -1)]
where the time goes in v1:
time: 190 us; the launch traced here: 188 us
  local copies, waits for them, and re-layouts  63.8 us (34%)
  starting transfers between devices  41.8 us (22%)
  other arithmetic  41.7 us (22%)
  waiting for transfers between devices  26.2 us (14%)
  matrix products  8.67 us (5%)
  between operations  5.93 us (3%)
    ppermute x8, starting transfers between devices, passed_along(): return lax.ppermute(block, axis, route)  24.4 us
    gather x16, local copies, waits for them, and re-layouts, pick(): return [jnp.take(wide, positions[j], axis=0) * masks[j] for j in range(4)]  21.4 us
    unnamed x86, local copies, waits for them, and re-layouts  16.5 us
    mul x16, other arithmetic, pick(): return [jnp.take(wide, positions[j], axis=0) * masks[j] for j in range(4)]  13.9 us
    all_to_all x2, waiting for transfers between devices, slope(): lax.all_to_all(left_cols, 'col', split_axis=2, concat_axis=3, tiled=True)  13.8 us
    add x8, other arithmetic, combine(): rise * upward[:, 0] + fall * (real * downward[:, 0] - imag * downward[:, 1])  11.9 us
    all_to_all x2, starting transfers between devices, slope(): lax.all_to_all(left_cols, 'col', split_axis=2, concat_axis=3, tiled=True)  9.21 us
    ppermute x8, waiting for transfers between devices, passed_along(): return lax.ppermute(block, axis, route)  8.95 us
  transfers between devices with their start and end apart: 12, of which 6 were waited for; matrix products, arithmetic and copies ran while one was open for 21% of the time, Pallas kernels for 0%

profile of v1, /device:TPU:3, one launch (start us, length us, event | category | flops | bytes accessed | tf_op | source)
XLA Modules:
  0.0 188.2 jit_solution(12794123460663514551)
XLA Ops:
  0.0 1.4 slice_bitcast_fusion.9
  1.5 1.4 reshape.406
  3.0 4.7 %all-to-all-start = ((f32[4,1,32768]{2,1,0:T(1,128)}), f32[4,1,32768]{2,1,0:T(1,128)S(1)}, u32[]{:S(2)}, u32[]{:S(2)}) async-start(f32[4,1,32768]{2,1,0:T(1,128)} %reshape.406), calls=%async_computation | async-start | bytes 1048576 | tf_op jit(solution)/shard_map/all_to_all | solution.py:83
  9.9 4.0 %collective-permute-start.2 = (f32[2,2,64,256]{3,2,1,0:T(8,128)S(1)}, f32[2,2,64,256]{3,2,1,0:T(8,128)S(1)}, u32[]{:S(2)}, u32[]{:S(2)}) collective-permute-start(f32[2,2,64,256]{3,2,1,0:T(8,128)S(1)} %get-tuple-element.61), channel_id=1, source_target_pairs={{0,4},{4,8},{8,12},{12,16},{16,20},{20,24},{24,28},{1,5},{5,9},{9,... | collective-permute-start | bytes 786440 | tf_op jit(solution)/shard_map/ppermute | solution.py:13
  13.9 1.9 %collective-permute-start.3 = (f32[2,2,64,256]{3,2,1,0:T(8,128)S(1)}, f32[2,2,64,256]{3,2,1,0:T(8,128)S(1)}, u32[]{:S(2)}, u32[]{:S(2)}) collective-permute-start(f32[2,2,64,256]{3,2,1,0:T(8,128)S(1)} %get-tuple-element.60), channel_id=1, source_target_pairs={{4,0},{8,4},{12,8},{16,12},{20,16},{24,20},{28,24},{5,1},{9,5},{13... | collective-permute-start | bytes 786440 | tf_op jit(solution)/shard_map/ppermute | solution.py:13
  24.1 1.4 gather_fusion.6
  26.1 2.2 %reduce = f32[4,32768]{1,0:T(4,128)S(1)} reduce(f32[4,1,32768]{2,1,0:T(1,128)S(1)} %all-to-all-done, f32[]{:T(128)} %broadcast.622), dimensions={1}, to_apply=%all_to_all.32.reduce_sub_computation | reduce | bytes 1048580 | tf_op jit(solution)/shard_map/all_to_all | solution.py:83
  30.1 1.8 reshape.223
  32.7 4.5 %collective-permute-start = (f32[2,2,256,64]{2,3,1,0:T(8,128)}, f32[2,2,256,64]{2,3,1,0:T(8,128)}, u32[]{:S(2)}, u32[]{:S(2)}) collective-permute-start(f32[2,2,256,64]{2,3,1,0:T(8,128)} %constant_dynamic-slice_fusion.2), channel_id=1, source_target_pairs={{0,4},{4,8},{8,12},{12,16},{16,20},{20,24},{24,28},{1,5},{5,9},{9,... | collective-permute-start | bytes 786440 | tf_op jit(solution)/shard_map/ppermute | solution.py:13
  37.3 2.0 %select_multiply_fusion.9 = f32[4,2,64,256]{3,2,1,0:T(8,128)} fusion(f32[4,2,64,256]{3,2,1,0:T(8,128)} %gather_fusion.6, f32[4]{0:T(128)S(1)} %get-tuple-element.81, pred[4]{0:T(512)(128)(4,1)S(1)} %get-tuple-element.76), kind=kLoop, calls=%fused_computation.82 | loop fusion | flops 262144 | bytes 1048596 | tf_op jit(solution)/shard_map/mul | solution.py:70
  39.2 1.4 gather_fusion.7
  41.5 1.3 copy.22
  43.1 1.9 %collective-permute-start.1 = (f32[2,2,256,64]{2,3,1,0:T(8,128)S(1)}, f32[2,2,256,64]{2,3,1,0:T(8,128)}, u32[]{:S(2)}, u32[]{:S(2)}) collective-permute-start(f32[2,2,256,64]{2,3,1,0:T(8,128)S(1)} %slice.195), channel_id=1, source_target_pairs={{4,0},{8,4},{12,8},{16,12},{20,16},{24,20},{28,24},{5,1},{9,5},{13... | collective-permute-start | bytes 786440 | tf_op jit(solution)/shard_map/ppermute | solution.py:13
  46.0 1.4 gather_fusion.4
  48.4 3.4 %collective-permute-done.1 = f32[2,2,256,64]{2,3,1,0:T(8,128)} collective-permute-done((f32[2,2,256,64]{2,3,1,0:T(8,128)S(1)}, f32[2,2,256,64]{2,3,1,0:T(8,128)}, u32[]{:S(2)}, u32[]{:S(2)}) %collective-permute-start.1) | collective-permute-done | bytes 262176 | tf_op jit(solution)/shard_map/ppermute | solution.py:13
  52.8 1.4 gather_fusion.2
  54.2 1.4 gather_fusion.3
  56.2 2.0 %select_multiply_fusion.13 = f32[4,2,256,64]{2,3,1,0:T(8,128)} fusion(f32[4,2,256,64]{2,3,1,0:T(8,128)} %gather_fusion.2, f32[4]{0:T(128)S(1)} %get-tuple-element.81, pred[4]{0:T(512)(128)(4,1)S(1)} %get-tuple-element.76), kind=kLoop, calls=%fused_computation.86 | loop fusion | flops 262144 | bytes 1048596 | tf_op jit(solution)/shard_map/mul | solution.py:70
  59.1 1.4 gather_fusion.1
  61.9 1.4 fusion.72
  63.3 1.4 fusion.74
  64.8 1.4 fusion.43
  67.0 1.9 %reshape.408 = f32[4,1,32768]{2,1,0:T(1,128)} reshape(f32[256,4,2,64]{3,2,1,0:T(2,128)S(1)} %bitcast.71) | data formatting | bytes 1048576
  68.9 4.9 %all-to-all-start.1 = ((f32[4,1,32768]{2,1,0:T(1,128)}), f32[4,1,32768]{2,1,0:T(1,128)}, u32[]{:S(2)}, u32[]{:S(2)}) async-start(f32[4,1,32768]{2,1,0:T(1,128)} %reshape.408), calls=%async_computation.1 | async-start | bytes 1048576 | tf_op jit(solution)/shard_map/all_to_all | solution.py:98
  74.0 1.4 gather_fusion.5
  76.6 1.6 fusion.68
  78.1 1.5 fusion.70
  79.7 6.6 %all-to-all-done.1 = f32[4,1,32768]{2,1,0:T(1,128)} async-done(((f32[4,1,32768]{2,1,0:T(1,128)}), f32[4,1,32768]{2,1,0:T(1,128)}, u32[]{:S(2)}, u32[]{:S(2)}) %all-to-all-start.1) | async-done | bytes 524320 | tf_op jit(solution)/shard_map/all_to_all | solution.py:98
  86.3 3.1 %reduce.1 = f32[4,32768]{1,0:T(4,128)S(1)} reduce(f32[4,1,32768]{2,1,0:T(1,128)} %all-to-all-done.1, f32[]{:T(128)} %broadcast.622), dimensions={1}, to_apply=%all_to_all.33.reduce_sub_computation | reduce | bytes 1048580 | tf_op jit(solution)/shard_map/all_to_all | solution.py:98
  92.1 2.4 %fusion.49 = f32[4,2,64,256]{3,2,1,0:T(8,128)S(1)} fusion(f32[4,2,64,256]{3,2,1,0:T(8,128)S(1)} %all_to_all.36, f32[4,1,64,256]{3,2,1,0:T(8,128)S(1)} %copy-done.29, f32[4,1,64,256]{3,2,1,0:T(8,128)S(1)} %copy-done.28, f32[4,1,64,256]{3,2,1,0:T(8,128)} %get-tuple-element.43, f32[4,1,64,256]{3,2,1,0:T(8,128)S(1)} %copy-done.30, ...), kind=kOutput, calls=%fused_computation.59 | convolution fusion | flops 1210056704 | bytes 3407872 | tf_op jit(solution)/shard_map/scij,jk->scik/dot_general | solution.py:94
  95.1 1.4 reshape.410
  96.5 3.5 %all-to-all-start.2 = ((f32[4,1,32768]{2,1,0:T(1,128)}), f32[4,1,32768]{2,1,0:T(1,128)S(1)}, u32[]{:S(2)}, u32[]{:S(2)}) async-start(f32[4,1,32768]{2,1,0:T(1,128)} %reshape.410), calls=%async_computation.2 | async-start | bytes 1048576 | tf_op jit(solution)/shard_map/all_to_all | solution.py:83
  100.1 1.9 %collective-permute-start.7 = (f32[2,2,64,256]{3,2,1,0:T(8,128)S(1)}, f32[2,2,64,256]{3,2,1,0:T(8,128)S(1)}, u32[]{:S(2)}, u32[]{:S(2)}) collective-permute-start(f32[2,2,64,256]{3,2,1,0:T(8,128)S(1)} %get-tuple-element.55), channel_id=1, source_target_pairs={{4,0},{8,4},{12,8},{16,12},{20,16},{24,20},{28,24},{5,1},{9,5},{13... | collective-permute-start | bytes 786440 | tf_op jit(solution)/shard_map/ppermute | solution.py:13
  102.0 4.5 %collective-permute-start.6 = (f32[2,2,64,256]{3,2,1,0:T(8,128)S(1)}, f32[2,2,64,256]{3,2,1,0:T(8,128)S(1)}, u32[]{:S(2)}, u32[]{:S(2)}) collective-permute-start(f32[2,2,64,256]{3,2,1,0:T(8,128)S(1)} %get-tuple-element.54), channel_id=1, source_target_pairs={{0,4},{4,8},{8,12},{12,16},{16,20},{20,24},{24,28},{1,5},{5,9},{9,... | collective-permute-start | bytes 786440 | tf_op jit(solution)/shard_map/ppermute | solution.py:13
  106.5 3.4 %collective-permute-done.7 = f32[2,2,64,256]{3,2,1,0:T(8,128)S(1)} collective-permute-done((f32[2,2,64,256]{3,2,1,0:T(8,128)S(1)}, f32[2,2,64,256]{3,2,1,0:T(8,128)S(1)}, u32[]{:S(2)}, u32[]{:S(2)}) %collective-permute-start.7) | collective-permute-done | bytes 262176 | tf_op jit(solution)/shard_map/ppermute | solution.py:13
  110.0 1.4 gather_fusion.14
  111.4 3.5 %all-to-all-done.2 = f32[4,1,32768]{2,1,0:T(1,128)S(1)} async-done(((f32[4,1,32768]{2,1,0:T(1,128)}), f32[4,1,32768]{2,1,0:T(1,128)S(1)}, u32[]{:S(2)}, u32[]{:S(2)}) %all-to-all-start.2) | async-done | bytes 524320 | tf_op jit(solution)/shard_map/all_to_all | solution.py:83
  114.9 3.0 %reduce.2 = f32[4,32768]{1,0:T(4,128)} reduce(f32[4,1,32768]{2,1,0:T(1,128)S(1)} %all-to-all-done.2, f32[]{:T(128)} %broadcast.622), dimensions={1}, to_apply=%all_to_all.37.reduce_sub_computation | reduce | bytes 1048580 | tf_op jit(solution)/shard_map/all_to_all | solution.py:83
  117.9 1.6 reshape.411
  120.8 2.6 %reshape.227 = f32[4,2,256,64]{2,3,1,0:T(8,128)} reshape(f32[4,2,4,64,64]{3,2,4,1,0:T(4,128)} %copy.25) | data formatting | bytes 1048576 | tf_op jit(solution)/shard_map/reshape | solution.py:84
  123.4 1.7 constant_dynamic-slice_fusion
  125.1 3.4 %collective-permute-start.4 = (f32[2,2,256,64]{2,3,1,0:T(8,128)}, f32[2,2,256,64]{2,3,1,0:T(8,128)}, u32[]{:S(2)}, u32[]{:S(2)}) collective-permute-start(f32[2,2,256,64]{2,3,1,0:T(8,128)} %constant_dynamic-slice_fusion), channel_id=1, source_target_pairs={{0,4},{4,8},{8,12},{12,16},{16,20},{20,24},{24,28},{1,5},{5,9},{9,... | collective-permute-start | bytes 786440 | tf_op jit(solution)/shard_map/ppermute | solution.py:13
  128.5 2.0 %select_multiply_fusion.1 = f32[4,2,64,256]{3,2,1,0:T(8,128)} fusion(f32[4,2,64,256]{3,2,1,0:T(8,128)} %gather_fusion.14, f32[4]{0:T(128)S(1)} %get-tuple-element.81, pred[4]{0:T(512)(128)(4,1)S(1)} %get-tuple-element.76), kind=kLoop, calls=%fused_computation.74 | loop fusion | flops 262144 | bytes 1048596 | tf_op jit(solution)/shard_map/mul | solution.py:70
  130.5 1.4 gather_fusion.15
  132.7 1.3 copy.26
  134.4 2.1 %collective-permute-start.5 = (f32[2,2,256,64]{2,3,1,0:T(8,128)S(1)}, f32[2,2,256,64]{2,3,1,0:T(8,128)}, u32[]{:S(2)}, u32[]{:S(2)}) collective-permute-start(f32[2,2,256,64]{2,3,1,0:T(8,128)S(1)} %slice.226), channel_id=1, source_target_pairs={{4,0},{8,4},{12,8},{16,12},{20,16},{24,20},{28,24},{5,1},{9,5},{13... | collective-permute-start | bytes 786440 | tf_op jit(solution)/shard_map/ppermute | solution.py:13
  137.5 1.4 gather_fusion.12
  140.9 2.2 %collective-permute-done.5 = f32[2,2,256,64]{2,3,1,0:T(8,128)} collective-permute-done((f32[2,2,256,64]{2,3,1,0:T(8,128)S(1)}, f32[2,2,256,64]{2,3,1,0:T(8,128)}, u32[]{:S(2)}, u32[]{:S(2)}) %collective-permute-start.5) | collective-permute-done | bytes 262176 | tf_op jit(solution)/shard_map/ppermute | solution.py:13
  144.1 1.4 gather_fusion.10
  145.5 1.4 gather_fusion.11
  146.8 1.4 gather_fusion.8
  148.2 1.4 gather_fusion.9
  152.1 1.4 fusion.63
  153.5 1.4 fusion.65
  155.0 2.2 %fusion.40 = f32[4,2,256,64]{2,3,1,0:T(8,128)} fusion(f32[4,1,256,64]{2,3,1,0:T(8,128)S(1)} %get-tuple-element.41, f32[4,1,256,64]{2,3,1,0:T(8,128)S(1)} %get-tuple-element.40, f32[4,1,256,64]{2,3,1,0:T(8,128)S(1)} %get-tuple-element.39, f32[4,1,256,64]{2,3,1,0:T(8,128)S(1)} %get-tuple-element.38, f32[4,2,256,64]{2,3,1,0:T(8,128)S(1)} %copy-done.6, ...), kind=kOutput, calls=%fused_computation.56 | convolution fusion | flops 1209925632 | bytes 2883584 | tf_op jit(solution)/shard_map/ij,scjk->scik/dot_general | solution.py:97
  157.2 1.7 copy.27
  158.9 1.9 %reshape.412 = f32[4,1,32768]{2,1,0:T(1,128)} reshape(f32[256,4,2,64]{3,2,1,0:T(2,128)S(1)} %bitcast.72) | data formatting | bytes 1048576
  160.8 4.3 %all-to-all-start.3 = ((f32[4,1,32768]{2,1,0:T(1,128)}), f32[4,1,32768]{2,1,0:T(1,128)}, u32[]{:S(2)}, u32[]{:S(2)}) async-start(f32[4,1,32768]{2,1,0:T(1,128)} %reshape.412), calls=%async_computation.3 | async-start | bytes 1048576 | tf_op jit(solution)/shard_map/all_to_all | solution.py:98
  166.0 1.4 gather_fusion.13
  168.6 1.6 fusion.59
  170.2 1.5 fusion.61
  171.7 7.2 %all-to-all-done.3 = f32[4,1,32768]{2,1,0:T(1,128)} async-done(((f32[4,1,32768]{2,1,0:T(1,128)}), f32[4,1,32768]{2,1,0:T(1,128)}, u32[]{:S(2)}, u32[]{:S(2)}) %all-to-all-start.3) | async-done | bytes 524320 | tf_op jit(solution)/shard_map/all_to_all | solution.py:98
  178.9 3.1 %reduce.3 = f32[4,32768]{1,0:T(4,128)S(1)} reduce(f32[4,1,32768]{2,1,0:T(1,128)} %all-to-all-done.3, f32[]{:T(128)} %broadcast.622), dimensions={1}, to_apply=%all_to_all.38.reduce_sub_computation | reduce | bytes 1048580 | tf_op jit(solution)/shard_map/all_to_all | solution.py:98
  184.5 2.6 %fusion.46 = f32[4,2,64,256]{3,2,1,0:T(8,128)S(1)} fusion(f32[4,2,64,256]{3,2,1,0:T(8,128)S(1)} %all_to_all.41, f32[4,1,64,256]{3,2,1,0:T(8,128)} %get-tuple-element.37, f32[4,1,64,256]{3,2,1,0:T(8,128)S(1)} %copy-done.27, f32[4,1,64,256]{3,2,1,0:T(8,128)} %get-tuple-element.35, f32[4,1,64,256]{3,2,1,0:T(8,128)} %get-tuple-element.34, ...), kind=kOutput, calls=%fused_computation.58 | convolution fusion | flops 1210056704 | bytes 3407872 | tf_op jit(solution)/shard_map/scij,jk->scik/dot_general | solution.py:94
  (149 shorter events, 35.4 us)
Async XLA Ops:
  1.5 6.2 %copy-start.31 = (s32[8]{0:T(128)S(1)}, s32[8]{0:T(128)}, u32[]{:S(2)}) copy-start(s32[8]{0:T(128)} %param.15) | copy-start | bytes 100
  1.5 8.3 %copy-start = (f32[4,2,64,256]{3,2,1,0:T(8,128)S(1)}, f32[4,2,64,256]{3,2,1,0:T(8,128)}, u32[]{:S(2)}) copy-start(f32[4,2,64,256]{3,2,1,0:T(8,128)} %param.10) | copy-start | bytes 1572868
  3.0 15.7 %copy-start.33 = (f32[2]{0:T(128)S(1)}, f32[2]{0:T(128)}, u32[]{:S(2)}) copy-start(f32[2]{0:T(128)} %param.13) | copy-start | bytes 28
  3.0 18.2 %copy-start.20 = (f32[2,256,256]{2,1,0:T(8,128)S(1)}, f32[2,256,256]{2,1,0:T(8,128)}, u32[]{:S(2)}) copy-start(f32[2,256,256]{2,1,0:T(8,128)} %param.12) | copy-start | bytes 1572868
  3.0 22.5 %all-to-all-start = ((f32[4,1,32768]{2,1,0:T(1,128)}), f32[4,1,32768]{2,1,0:T(1,128)S(1)}, u32[]{:S(2)}, u32[]{:S(2)}) async-start(f32[4,1,32768]{2,1,0:T(1,128)} %reshape.406), calls=%async_computation | async-start | bytes 1048576 | tf_op jit(solution)/shard_map/all_to_all | solution.py:83
  9.9 12.2 %copy-start.32 = (f32[2,2]{1,0:T(2,128)S(1)}, f32[2,2]{1,0:T(2,128)}, u32[]{:S(2)}) copy-start(f32[2,2]{1,0:T(2,128)} %param.14) | copy-start | bytes 52
  9.9 14.0 %collective-permute-start.2 = (f32[2,2,64,256]{3,2,1,0:T(8,128)S(1)}, f32[2,2,64,256]{3,2,1,0:T(8,128)S(1)}, u32[]{:S(2)}, u32[]{:S(2)}) collective-permute-start(f32[2,2,64,256]{3,2,1,0:T(8,128)S(1)} %get-tuple-element.61), channel_id=1, source_target_pairs={{0,4},{4,8},{8,12},{12,16},{16,20},{20,24},{24,28},{1,5},{5,9},{9,... | collective-permute-start | bytes 786440 | tf_op jit(solution)/shard_map/ppermute | solution.py:13
  13.9 10.1 %collective-permute-start.3 = (f32[2,2,64,256]{3,2,1,0:T(8,128)S(1)}, f32[2,2,64,256]{3,2,1,0:T(8,128)S(1)}, u32[]{:S(2)}, u32[]{:S(2)}) collective-permute-start(f32[2,2,64,256]{3,2,1,0:T(8,128)S(1)} %get-tuple-element.60), channel_id=1, source_target_pairs={{4,0},{8,4},{12,8},{16,12},{20,16},{24,20},{28,24},{5,1},{9,5},{13... | collective-permute-start | bytes 786440 | tf_op jit(solution)/shard_map/ppermute | solution.py:13
  31.9 16.5 %copy-start.7 = (f32[4,2,256,64]{2,3,1,0:T(8,128)}, f32[4,2,256,64]{2,3,1,0:T(8,128)S(1)}, u32[]{:S(2)}) copy-start(f32[4,2,256,64]{2,3,1,0:T(8,128)S(1)} %reshape.223) | copy-start | bytes 1572868
  32.7 14.7 %collective-permute-start = (f32[2,2,256,64]{2,3,1,0:T(8,128)}, f32[2,2,256,64]{2,3,1,0:T(8,128)}, u32[]{:S(2)}, u32[]{:S(2)}) collective-permute-start(f32[2,2,256,64]{2,3,1,0:T(8,128)} %constant_dynamic-slice_fusion.2), channel_id=1, source_target_pairs={{0,4},{4,8},{8,12},{12,16},{16,20},{20,24},{24,28},{1,5},{5,9},{9,... | collective-permute-start | bytes 786440 | tf_op jit(solution)/shard_map/ppermute | solution.py:13
  41.5 3.6 %copy-start.18 = (f32[4,2,64,256]{3,2,1,0:T(8,128)S(1)}, f32[4,2,64,256]{3,2,1,0:T(8,128)}, u32[]{:S(2)}) copy-start(f32[4,2,64,256]{3,2,1,0:T(8,128)} %gather_fusion.7) | copy-start | bytes 1572868
  43.1 8.7 %collective-permute-start.1 = (f32[2,2,256,64]{2,3,1,0:T(8,128)S(1)}, f32[2,2,256,64]{2,3,1,0:T(8,128)}, u32[]{:S(2)}, u32[]{:S(2)}) collective-permute-start(f32[2,2,256,64]{2,3,1,0:T(8,128)S(1)} %slice.195), channel_id=1, source_target_pairs={{4,0},{8,4},{12,8},{16,12},{20,16},{24,20},{28,24},{5,1},{9,5},{13... | collective-permute-start | bytes 786440 | tf_op jit(solution)/shard_map/ppermute | solution.py:13
  56.2 2.0 %copy-start.5 = (f32[4,2,256,64]{2,3,1,0:T(8,128)S(1)}, f32[4,2,256,64]{2,3,1,0:T(8,128)}, u32[]{:S(2)}) copy-start(f32[4,2,256,64]{2,3,1,0:T(8,128)} %gather_fusion.3) | copy-start | bytes 1572868
  60.5 1.0 copy-start.4
  60.5 1.2 copy-start.14
  60.5 1.4 copy-start.15
  63.3 1.5 copy-start.8
  63.3 1.5 copy-start.21
  63.3 1.5 copy-start.23
  63.3 1.5 copy-start.34
  68.9 4.9 %copy-start.17 = (f32[4,2,64,256]{3,2,1,0:T(8,128)S(1)}, f32[4,2,64,256]{3,2,1,0:T(8,128)}, u32[]{:S(2)}) copy-start(f32[4,2,64,256]{3,2,1,0:T(8,128)} %gather_fusion.4) | copy-start | bytes 1572868
  68.9 17.4 %all-to-all-start.1 = ((f32[4,1,32768]{2,1,0:T(1,128)}), f32[4,1,32768]{2,1,0:T(1,128)}, u32[]{:S(2)}, u32[]{:S(2)}) async-start(f32[4,1,32768]{2,1,0:T(1,128)} %reshape.408), calls=%async_computation.1 | async-start | bytes 1048576 | tf_op jit(solution)/shard_map/all_to_all | solution.py:98
  74.0 2.6 %copy-start.11 = (f32[4,2,64,256]{3,2,1,0:T(8,128)S(1)}, f32[4,2,64,256]{3,2,1,0:T(8,128)}, u32[]{:S(2)}) copy-start(f32[4,2,64,256]{3,2,1,0:T(8,128)} %select_multiply_fusion.9) | copy-start | bytes 1572868
  74.0 2.6 %copy-start.12 = (f32[4,2,64,256]{3,2,1,0:T(8,128)S(1)}, f32[4,2,64,256]{3,2,1,0:T(8,128)}, u32[]{:S(2)}) copy-start(f32[4,2,64,256]{3,2,1,0:T(8,128)} %select_multiply_fusion.8) | copy-start | bytes 1572868
  90.9 1.0 copy-start.24
  90.9 1.0 copy-start.28
  90.9 1.1 copy-start.29
  90.9 1.2 copy-start.30
  96.5 18.4 %all-to-all-start.2 = ((f32[4,1,32768]{2,1,0:T(1,128)}), f32[4,1,32768]{2,1,0:T(1,128)S(1)}, u32[]{:S(2)}, u32[]{:S(2)}) async-start(f32[4,1,32768]{2,1,0:T(1,128)} %reshape.410), calls=%async_computation.2 | async-start | bytes 1048576 | tf_op jit(solution)/shard_map/all_to_all | solution.py:83
  100.1 9.8 %collective-permute-start.7 = (f32[2,2,64,256]{3,2,1,0:T(8,128)S(1)}, f32[2,2,64,256]{3,2,1,0:T(8,128)S(1)}, u32[]{:S(2)}, u32[]{:S(2)}) collective-permute-start(f32[2,2,64,256]{3,2,1,0:T(8,128)S(1)} %get-tuple-element.55), channel_id=1, source_target_pairs={{4,0},{8,4},{12,8},{16,12},{20,16},{24,20},{28,24},{5,1},{9,5},{13... | collective-permute-start | bytes 786440 | tf_op jit(solution)/shard_map/ppermute | solution.py:13
  102.0 7.9 %collective-permute-start.6 = (f32[2,2,64,256]{3,2,1,0:T(8,128)S(1)}, f32[2,2,64,256]{3,2,1,0:T(8,128)S(1)}, u32[]{:S(2)}, u32[]{:S(2)}) collective-permute-start(f32[2,2,64,256]{3,2,1,0:T(8,128)S(1)} %get-tuple-element.54), channel_id=1, source_target_pairs={{0,4},{4,8},{8,12},{12,16},{16,20},{20,24},{24,28},{1,5},{5,9},{9,... | collective-permute-start | bytes 786440 | tf_op jit(solution)/shard_map/ppermute | solution.py:13
  125.1 13.8 %collective-permute-start.4 = (f32[2,2,256,64]{2,3,1,0:T(8,128)}, f32[2,2,256,64]{2,3,1,0:T(8,128)}, u32[]{:S(2)}, u32[]{:S(2)}) collective-permute-start(f32[2,2,256,64]{2,3,1,0:T(8,128)} %constant_dynamic-slice_fusion), channel_id=1, source_target_pairs={{0,4},{4,8},{8,12},{12,16},{16,20},{20,24},{24,28},{1,5},{5,9},{9,... | collective-permute-start | bytes 786440 | tf_op jit(solution)/shard_map/ppermute | solution.py:13
  132.7 3.8 %copy-start.19 = (f32[4,2,64,256]{3,2,1,0:T(8,128)S(1)}, f32[4,2,64,256]{3,2,1,0:T(8,128)}, u32[]{:S(2)}) copy-start(f32[4,2,64,256]{3,2,1,0:T(8,128)} %gather_fusion.15) | copy-start | bytes 1572868
  134.4 8.7 %collective-permute-start.5 = (f32[2,2,256,64]{2,3,1,0:T(8,128)S(1)}, f32[2,2,256,64]{2,3,1,0:T(8,128)}, u32[]{:S(2)}, u32[]{:S(2)}) collective-permute-start(f32[2,2,256,64]{2,3,1,0:T(8,128)S(1)} %slice.226), channel_id=1, source_target_pairs={{4,0},{8,4},{12,8},{16,12},{20,16},{24,20},{28,24},{5,1},{9,5},{13... | collective-permute-start | bytes 786440 | tf_op jit(solution)/shard_map/ppermute | solution.py:13
  149.6 1.3 copy-start.1
  149.6 1.4 copy-start.2
  150.9 1.1 copy-start.3
  153.5 1.5 copy-start.6
  153.5 1.5 copy-start.22
  153.5 1.5 copy-start.25
  153.5 1.5 copy-start.35
  160.8 4.3 %copy-start.16 = (f32[4,2,64,256]{3,2,1,0:T(8,128)S(1)}, f32[4,2,64,256]{3,2,1,0:T(8,128)}, u32[]{:S(2)}) copy-start(f32[4,2,64,256]{3,2,1,0:T(8,128)} %gather_fusion.12) | copy-start | bytes 1572868
  160.8 18.1 %all-to-all-start.3 = ((f32[4,1,32768]{2,1,0:T(1,128)}), f32[4,1,32768]{2,1,0:T(1,128)}, u32[]{:S(2)}, u32[]{:S(2)}) async-start(f32[4,1,32768]{2,1,0:T(1,128)} %reshape.412), calls=%async_computation.3 | async-start | bytes 1048576 | tf_op jit(solution)/shard_map/all_to_all | solution.py:98
  166.0 2.6 %copy-start.9 = (f32[4,2,64,256]{3,2,1,0:T(8,128)S(1)}, f32[4,2,64,256]{3,2,1,0:T(8,128)}, u32[]{:S(2)}) copy-start(f32[4,2,64,256]{3,2,1,0:T(8,128)} %select_multiply_fusion.1) | copy-start | bytes 1572868
  166.0 2.6 %copy-start.10 = (f32[4,2,64,256]{3,2,1,0:T(8,128)S(1)}, f32[4,2,64,256]{3,2,1,0:T(8,128)}, u32[]{:S(2)}) copy-start(f32[4,2,64,256]{3,2,1,0:T(8,128)} %select_multiply_fusion) | copy-start | bytes 1572868
  168.6 1.6 copy-start.13
  183.5 1.0 copy-start.26
  183.5 1.0 copy-start.27
